TPU v7x, 256 devices: a whole 4x4x8 slice. The times are simulated.
256 devices in a mesh: leaf: 32 (over z, y), front: 8 (over x, core).
Axes of the slice: x: 4, y: 4, z: 8, core: 2. Of those that a mesh axis runs over, the one named last changes fastest.
Arguments:
- section_updates: bfloat16 [32768, 256], P(('leaf', 'front')), may hold values from -6 to 6
- upper_rhs: float32 [126976, 256], P(('leaf', 'front')), may hold values from -6 to 6
- pivot_inverse: bfloat16 [126976, 4096], P('leaf', 'front'), may hold values from -0.09375 to 0.09375
- coupling: bfloat16 [1024, 122880], P('front', 'leaf'), may hold values from -0.09375 to 0.09375
- extend_lists: int32 [62, 8], replicated, may hold values from 0 to 39, as said below
Outputs:
- solution: float32 [126976, 256], P(('leaf', 'front'))
- interface: bfloat16 [32768, 256], P(('leaf', 'front'))
Inputs may be any that keep to these rules, and one draw needn't show every extreme that they name: `extend_lists`: each row names 8 different blocks of the parent's frame; the rows of the root's two children name pivot blocks only, below 32.
All inputs are finite; a program needn't handle non-finite values.
Results may differ from a plain program's by a relative error of at most 0.022.
Values may be sent and summed in bfloat16 or wider, within the bound.
A program may use at most 64 MiB of HBM per device.

v0:
```python
import jax
import jax.numpy as jnp
from jax import lax
from jax.sharding import PartitionSpec as P

PIV = 4096
UPD = 1024
BLK = 128


def partner(block, axis, stride):
    count = lax.axis_size(axis)
    route = []
    for low in range(count):
        high = low | 1 << stride
        if high != low and high < count:
            route += [(low, high), (high, low)]
    return lax.ppermute(block, axis, route)


def child_base(leaves, height):
    total_rows = 0
    for depth in range(height - 1):
        total_rows = total_rows + leaves // 2**depth
    return total_rows


def list_row(extend_lists, row_index):
    return lax.dynamic_slice_in_dim(extend_lists, row_index, 1, 0)[0]


def upper_bit(position, bit_index):
    return position >> bit_index & 1 == 1


def joined(position, bit_index, portion, partner_rows):
    return jnp.where(
        upper_bit(position, bit_index),
        jnp.concatenate([partner_rows, portion], 0),
        jnp.concatenate([portion, partner_rows], 0),
    )


def gather_own(portion, height, position):
    for bit_index in range(height):
        partner_rows = partner(portion.astype(jnp.bfloat16), "leaf", bit_index).astype(
            portion.dtype
        )
        portion = joined(position, bit_index, portion, partner_rows)
    return portion


def sum_updates(summand, height):
    for bit_index in range(height):
        summand = summand + partner(summand.astype(jnp.bfloat16), "leaf", bit_index).astype(
            summand.dtype
        )
    return summand


def sum_solution(summand, height):
    for bit_index in range(height):
        summand = summand + partner(summand.astype(jnp.bfloat16), "leaf", bit_index).astype(
            summand.dtype
        )
    return summand


def per_device(section_updates, upper_rhs, pivot_inverse, coupling, extend_lists):
    leaves = lax.axis_size("leaf")
    fronts = lax.axis_size("front")
    levels = leaves.bit_length() - 1
    position = lax.axis_index("leaf")
    column = lax.axis_index("front")
    rhs_width = upper_rhs.shape[1]
    piv_dev = PIV // fronts
    upd_dev = UPD // fronts
    piv_blocks = piv_dev // BLK
    upd_blocks = upd_dev // BLK
    block_count = UPD // BLK
    local_blocks = jnp.concatenate(
        [
            column * piv_blocks + jnp.arange(piv_blocks, dtype=jnp.int32),
            PIV // BLK + column * upd_blocks + jnp.arange(upd_blocks, dtype=jnp.int32),
        ]
    )
    local_count = piv_blocks + upd_blocks
    carried = section_updates
    saved_part = []
    saved_half = []
    for height in range(1, levels + 1):
        group_size = 2**height
        span_rows = PIV // group_size
        band_start = PIV - PIV // 2 ** (height - 1)
        rhs_len = piv_dev // group_size
        rhs_start = piv_dev - piv_dev // 2 ** (height - 1)
        member = position & group_size - 1
        own_child = child_base(leaves, height) + (position >> height - 1)
        sibling = partner(carried, "leaf", height - 1)
        pair_blocks = lax.all_gather(jnp.stack([carried, sibling]), "front", axis=1, tiled=True)
        pair_lists = jnp.stack(
            [list_row(extend_lists, own_child), list_row(extend_lists, own_child ^ 1)]
        )
        chooser = (pair_lists.reshape(2 * block_count)[None, :] == local_blocks[:, None]).astype(
            jnp.bfloat16
        )
        assembled = jnp.dot(
            chooser,
            pair_blocks.reshape(2 * block_count, BLK * rhs_width),
            preferred_element_type=jnp.float32,
        ).reshape(local_count * BLK, rhs_width)
        own_rows = gather_own(upper_rhs[rhs_start : rhs_start + rhs_len], height, position)
        rows_half = (own_rows + assembled[:piv_dev]).astype(jnp.bfloat16)
        g_share = pivot_inverse[band_start : band_start + span_rows]
        pivot_part = lax.psum(
            jnp.dot(g_share, rows_half, preferred_element_type=jnp.float32).astype(jnp.bfloat16),
            "front",
        ).astype(jnp.float32)
        pivot_half = pivot_part.astype(jnp.bfloat16)
        saved_part.append(pivot_part)
        saved_half.append(pivot_half)
        if height < levels:
            c_share = coupling[:, band_start : band_start + span_rows]
            summand = jnp.dot(c_share, pivot_half, preferred_element_type=jnp.float32)
            frame_upd = assembled[piv_dev:]
            carried = (frame_upd - sum_updates(summand, height)).astype(jnp.bfloat16)
    from_above = carried
    outputs = []
    for height in range(levels, 0, -1):
        group_size = 2**height
        span_rows = PIV // group_size
        band_start = PIV - PIV // 2 ** (height - 1)
        member = position & group_size - 1
        pivot_part = saved_part[height - 1]
        if height < levels:
            c_share = coupling[:, band_start : band_start + span_rows]
            back_total = lax.psum(
                jnp.einsum(
                    "up,ur->pr", c_share, from_above, preferred_element_type=jnp.float32
                ).astype(jnp.bfloat16),
                "front",
            ).astype(jnp.float32)
            weight_half = (pivot_part - back_total).astype(jnp.bfloat16)
            upper_rows = from_above
        else:
            weight_half = saved_half[height - 1]
            upper_rows = jnp.zeros((upd_dev, rhs_width), jnp.bfloat16)
        g_share = pivot_inverse[band_start : band_start + span_rows]
        solve_term = jnp.einsum(
            "cp,cr->pr", g_share, weight_half, preferred_element_type=jnp.float32
        )
        part_len = piv_dev // group_size
        summed = sum_solution(solve_term, height)
        portion = lax.dynamic_slice_in_dim(summed, member * part_len, part_len, 0)
        rows_half = summed.astype(jnp.bfloat16)
        outputs.append(portion)
        frame_half = jnp.concatenate([rows_half, upper_rows], 0).reshape(
            local_count, BLK * rhs_width
        )
        child_list = list_row(extend_lists, child_base(leaves, height) + (position >> height - 1))
        picker = (child_list[:, None] == local_blocks[None, :]).astype(jnp.bfloat16)
        outgoing = (
            jnp.dot(picker, frame_half, preferred_element_type=jnp.float32)
            .astype(jnp.bfloat16)
            .reshape(fronts, upd_dev, rhs_width)
        )
        incoming = lax.all_to_all(outgoing, "front", split_axis=0, concat_axis=0, tiled=True)
        from_above = jnp.sum(incoming, axis=0, dtype=jnp.float32).astype(jnp.bfloat16)
    solution = jnp.concatenate(outputs[::-1], 0)
    return (solution, from_above)


def solution(mesh):
    placed = (
        P(("leaf", "front"), None),
        P(("leaf", "front"), None),
        P("leaf", "front"),
        P("front", "leaf"),
        P(),
    )
    return jax.shard_map(
        per_device,
        mesh=mesh,
        in_specs=placed,
        out_specs=(P(("leaf", "front"), None), P(("leaf", "front"), None)),
        check_vma=False,
    )
```

profile of v0, /device:TPU:1, one launch (start us, length us, event | category | flops | bytes accessed | tf_op | source)
XLA Modules:
  0.0 1092.0 jit_solution(5823587160174523353)
XLA Ops:
  18.5 25.0 %all-gather.6.cloned.1.call-done = bf16[2,1024,256]{2,1,0:T(8,128)(2,1)} async-done(((bf16[2,128,256]{2,1,0:T(8,128)(2,1)}), bf16[2,1024,256]{2,1,0:T(8,128)(2,1)}) %all-gather.6.cloned.1.call-update) | async-done | bytes 1048592 | tf_op jit(solution)/shard_map/all_gather | solution.py:100
  49.5 65.4 %all-reduce.11.cloned.1.call-done = bf16[2048,256]{0,1:T(8,128)(2,1)} async-done(((bf16[2048,256]{0,1:T(8,128)(2,1)}), bf16[2048,256]{0,1:T(8,128)(2,1)}) %all-reduce.11.cloned.1.call-update) | async-done | bytes 1048592 | tf_op jit(solution)/shard_map/psum | solution.py:115
  135.2 20.1 %all-gather.8.cloned.1.call-done = bf16[2,1024,256]{1,2,0:T(8,128)(2,1)} async-done(((bf16[2,128,256]{1,2,0:T(8,128)(2,1)}), bf16[2,1024,256]{1,2,0:T(8,128)(2,1)}) %all-gather.8.cloned.1.call-update) | async-done | bytes 1048592 | tf_op jit(solution)/shard_map/all_gather | solution.py:100
  161.8 64.7 %all-reduce.13.cloned.1.call-done = bf16[1024,256]{0,1:T(8,128)(2,1)} async-done(((bf16[1024,256]{0,1:T(8,128)(2,1)}), bf16[1024,256]{0,1:T(8,128)(2,1)}) %all-reduce.13.cloned.1.call-update) | async-done | bytes 524304 | tf_op jit(solution)/shard_map/psum | solution.py:115
  252.5 18.5 %all-gather.10.cloned.1.call-done = bf16[2,1024,256]{1,2,0:T(8,128)(2,1)} async-done(((bf16[2,128,256]{1,2,0:T(8,128)(2,1)}), bf16[2,1024,256]{1,2,0:T(8,128)(2,1)}) %all-gather.10.cloned.1.call-update) | async-done | bytes 1048592 | tf_op jit(solution)/shard_map/all_gather | solution.py:100
  277.1 63.9 %all-reduce.15.cloned.1.call-done = bf16[512,256]{0,1:T(8,128)(2,1)} async-done(((bf16[512,256]{0,1:T(8,128)(2,1)}), bf16[512,256]{0,1:T(8,128)(2,1)}) %all-reduce.15.cloned.1.call-update) | async-done | bytes 262160 | tf_op jit(solution)/shard_map/psum | solution.py:115
  376.0 15.2 %all-gather.12.cloned.1.call-done = bf16[2,1024,256]{1,2,0:T(8,128)(2,1)} async-done(((bf16[2,128,256]{1,2,0:T(8,128)(2,1)}), bf16[2,1024,256]{1,2,0:T(8,128)(2,1)}) %all-gather.12.cloned.1.call-update) | async-done | bytes 1048592 | tf_op jit(solution)/shard_map/all_gather | solution.py:100
  397.1 63.6 %all-reduce.17.cloned.1.call-done = bf16[256,256]{0,1:T(8,128)(2,1)} async-done(((bf16[256,256]{0,1:T(8,128)(2,1)}), bf16[256,256]{0,1:T(8,128)(2,1)}) %all-reduce.17.cloned.1.call-update) | async-done | bytes 131088 | tf_op jit(solution)/shard_map/psum | solution.py:115
  477.2 6.3 collective-permute-start.29
  501.5 5.0 collective-permute-start.24
  509.4 11.0 %all-gather.14.cloned.1.call-done = bf16[2,1024,256]{1,2,0:T(8,128)(2,1)} async-done(((bf16[2,128,256]{1,2,0:T(8,128)(2,1)}), bf16[2,1024,256]{1,2,0:T(8,128)(2,1)}) %all-gather.14.cloned.1.call-update) | async-done | bytes 1048592 | tf_op jit(solution)/shard_map/all_gather | solution.py:100
  525.2 66.1 %all-reduce.19.cloned.1.call-done = bf16[128,256]{0,1:T(8,128)(2,1)} async-done(((bf16[128,256]{0,1:T(8,128)(2,1)}), bf16[128,256]{0,1:T(8,128)(2,1)}) %all-reduce.19.cloned.1.call-update) | async-done | bytes 65552 | tf_op jit(solution)/shard_map/psum | solution.py:115
  593.5 4.2 collective-permute-done.30
  600.4 5.5 collective-permute-done.31
  613.8 6.7 collective-permute-done.33
  620.6 5.5 collective-permute-start.34
  626.2 6.8 collective-permute-done.34
  634.9 30.3 %all_to_all.25 = bf16[8,128,256]{2,1,0:T(8,128)(2,1)S(1)} all-to-all(bf16[8,128,256]{2,1,0:T(8,128)(2,1)S(1)} %copy.50), channel_id=1, replica_groups=mesh['leaf'=32,'front'=8] {'front'}, dimensions={0} | all-to-all | bytes 1048576 | tf_op jit(solution)/shard_map/all_to_all | solution.py:167
  666.2 59.3 %all-reduce.21.cloned.1.call-done = bf16[256,256]{0,1:T(8,128)(2,1)} async-done(((bf16[256,256]{0,1:T(8,128)(2,1)}), bf16[256,256]{0,1:T(8,128)(2,1)}) %all-reduce.21.cloned.1.call-update) | async-done | bytes 131088 | tf_op jit(solution)/shard_map/psum | solution.py:137
  728.0 4.1 collective-permute-done.35
  734.9 5.4 collective-permute-done.36
  748.6 6.6 collective-permute-done.38
  757.2 24.9 %all_to_all.26 = bf16[8,128,256]{2,1,0:T(8,128)(2,1)S(1)} all-to-all(bf16[8,128,256]{2,1,0:T(8,128)(2,1)S(1)} %copy.54), channel_id=1, replica_groups=mesh['leaf'=32,'front'=8] {'front'}, dimensions={0} | all-to-all | bytes 1048576 | tf_op jit(solution)/shard_map/all_to_all | solution.py:167
  783.2 62.7 %all-reduce.23.cloned.1.call-done = bf16[512,256]{0,1:T(8,128)(2,1)} async-done(((bf16[512,256]{0,1:T(8,128)(2,1)}), bf16[512,256]{0,1:T(8,128)(2,1)}) %all-reduce.23.cloned.1.call-update) | async-done | bytes 262160 | tf_op jit(solution)/shard_map/psum | solution.py:137
  855.5 5.4 collective-permute-done.40
  868.3 20.9 %all_to_all.27 = bf16[8,128,256]{2,1,0:T(8,128)(2,1)S(1)} all-to-all(bf16[8,128,256]{2,1,0:T(8,128)(2,1)S(1)} %copy.58), channel_id=1, replica_groups=mesh['leaf'=32,'front'=8] {'front'}, dimensions={0} | all-to-all | bytes 1048576 | tf_op jit(solution)/shard_map/all_to_all | solution.py:167
  890.4 63.8 %all-reduce.25.cloned.1.call-done = bf16[1024,256]{0,1:T(8,128)(2,1)} async-done(((bf16[1024,256]{0,1:T(8,128)(2,1)}), bf16[1024,256]{0,1:T(8,128)(2,1)}) %all-reduce.25.cloned.1.call-update) | async-done | bytes 524304 | tf_op jit(solution)/shard_map/psum | solution.py:137
  964.4 5.2 collective-permute-done.43
  970.8 19.0 %all_to_all.28 = bf16[8,128,256]{2,1,0:T(8,128)(2,1)S(1)} all-to-all(bf16[8,128,256]{2,1,0:T(8,128)(2,1)S(1)} %copy.62), channel_id=1, replica_groups=mesh['leaf'=32,'front'=8] {'front'}, dimensions={0} | all-to-all | bytes 1048576 | tf_op jit(solution)/shard_map/all_to_all | solution.py:167
  991.3 65.7 %all-reduce.27.cloned.1.call-done = bf16[2048,256]{0,1:T(8,128)(2,1)} async-done(((bf16[2048,256]{0,1:T(8,128)(2,1)}), bf16[2048,256]{0,1:T(8,128)(2,1)}) %all-reduce.27.cloned.1.call-update) | async-done | bytes 1048592 | tf_op jit(solution)/shard_map/psum | solution.py:137
  1066.9 8.3 all-to-all-start.4
  1078.4 6.1 all-to-all-done.4
  (307 shorter events, 235.7 us)
Async XLA Ops:
  7.2 36.2 %all-gather.6.cloned.1.call-start = ((), (), s32[]{:S(2)}) async-start(), calls=%async_computation.5 | async-start | bytes 1179648 | tf_op jit(solution)/shard_map/all_gather | solution.py:100
  12.8 102.0 %all-reduce.11.cloned.1.call-start = ((), (), s32[]{:S(2)}) async-start(), calls=%async_computation.6 | async-start | bytes 2097152 | tf_op jit(solution)/shard_map/psum | solution.py:115
  49.5 105.8 %all-gather.8.cloned.1.call-start = ((), (), s32[]{:S(2)}) async-start(), calls=%async_computation.7 | async-start | bytes 1179648 | tf_op jit(solution)/shard_map/all_gather | solution.py:100
  125.3 101.3 %all-reduce.13.cloned.1.call-start = ((), (), s32[]{:S(2)}) async-start(), calls=%async_computation.8 | async-start | bytes 1048576 | tf_op jit(solution)/shard_map/psum | solution.py:115
  129.8 5.3 collective-permute-start.3
  161.7 109.2 %all-gather.10.cloned.1.call-start = ((), (), s32[]{:S(2)}) async-start(), calls=%async_computation.9 | async-start | bytes 1179648 | tf_op jit(solution)/shard_map/all_gather | solution.py:100
  239.7 101.2 %all-reduce.15.cloned.1.call-start = ((), (), s32[]{:S(2)}) async-start(), calls=%async_computation.10 | async-start | bytes 524288 | tf_op jit(solution)/shard_map/psum | solution.py:115
  277.0 114.2 %all-gather.12.cloned.1.call-start = ((), (), s32[]{:S(2)}) async-start(), calls=%async_computation.11 | async-start | bytes 1179648 | tf_op jit(solution)/shard_map/all_gather | solution.py:100
  358.2 102.5 %all-reduce.17.cloned.1.call-start = ((), (), s32[]{:S(2)}) async-start(), calls=%async_computation.12 | async-start | bytes 262144 | tf_op jit(solution)/shard_map/psum | solution.py:115
  369.3 6.6 collective-permute-start.15
  397.1 123.3 %all-gather.14.cloned.1.call-start = ((), (), s32[]{:S(2)}) async-start(), calls=%async_computation.13 | async-start | bytes 1179648 | tf_op jit(solution)/shard_map/all_gather | solution.py:100
  477.2 8.1 collective-permute-start.29
  485.9 105.4 %all-reduce.19.cloned.1.call-start = ((), (), s32[]{:S(2)}) async-start(), calls=%async_computation.14 | async-start | bytes 131072 | tf_op jit(solution)/shard_map/psum | solution.py:115
  501.5 7.8 collective-permute-start.24
  525.1 200.5 %all-reduce.21.cloned.1.call-start = ((), (), s32[]{:S(2)}) async-start(), calls=%async_computation.15 | async-start | bytes 262144 | tf_op jit(solution)/shard_map/psum | solution.py:137
  597.8 8.2 collective-permute-start.31
  606.1 5.3 collective-permute-start.32
  611.5 9.1 collective-permute-start.33
  620.6 12.3 %collective-permute-start.34 = (bf16[512,256]{0,1:T(8,128)(2,1)S(1)}, bf16[512,256]{0,1:T(8,128)(2,1)S(1)}, u32[]{:S(2)}, u32[]{:S(2)}) collective-permute-start(bf16[512,256]{0,1:T(8,128)(2,1)S(1)} %fusion.51), channel_id=1, source_target_pairs={{0,128},{128,0},{8,136},{136,8},{16,144},{144,16},{24,152},{152,24... | collective-permute-start | bytes 786440 | tf_op jit(solution)/shard_map/ppermute | solution.py:18
  666.2 179.7 %all-reduce.23.cloned.1.call-start = ((), (), s32[]{:S(2)}) async-start(), calls=%async_computation.16 | async-start | bytes 524288 | tf_op jit(solution)/shard_map/psum | solution.py:137
  726.8 5.3 collective-permute-start.35
  732.2 8.2 collective-permute-start.36
  740.5 5.3 collective-permute-start.37
  745.9 9.3 collective-permute-start.38
  783.1 171.1 %all-reduce.25.cloned.1.call-start = ((), (), s32[]{:S(2)}) async-start(), calls=%async_computation.17 | async-start | bytes 1048576 | tf_op jit(solution)/shard_map/psum | solution.py:137
  847.3 5.3 collective-permute-start.39
  852.7 8.2 collective-permute-start.40
  861.0 5.3 collective-permute-start.41
  890.4 166.6 %all-reduce.27.cloned.1.call-start = ((), (), s32[]{:S(2)}) async-start(), calls=%async_computation.18 | async-start | bytes 2097152 | tf_op jit(solution)/shard_map/psum | solution.py:137
  961.5 8.2 collective-permute-start.43
  1059.6 5.3 collective-permute-start.44
  1066.9 17.6 %all-to-all-start.4 = ((bf16[8,128,256]{2,1,0:T(8,128)(2,1)}), bf16[8,128,256]{2,1,0:T(8,128)(2,1)S(1)}, u32[]{:S(2)}, u32[]{:S(2)}) async-start(bf16[8,128,256]{2,1,0:T(8,128)(2,1)} %copy.66), calls=%async_computation.4 | async-start | bytes 1048576 | tf_op jit(solution)/shard_map/all_to_all | solution.py:167
  (43 other events, 1283.6 us)
Sparse Core Ops, SparseCore 0:
  12.9 30.4 all-gather.5
  49.6 65.2 all-reduce.10
  125.4 29.7 all-gather.7
  161.8 64.6 all-reduce.12
  239.9 31.0 all-gather.9
  277.1 63.8 all-reduce.14
  358.3 32.8 all-gather.11
  397.2 63.4 all-reduce.16
  486.0 34.3 all-gather.13
  525.2 66.0 all-reduce.18
  666.3 59.1 all-reduce.20
  783.3 62.6 all-reduce.22
  890.5 63.6 all-reduce.24
  991.4 65.4 all-reduce.26
where the time goes:
time: 1100 us; the launch traced here: 1090 us
  waiting for transfers between devices  799 us (73%)
  starting transfers between devices  105 us (10%)
  blocking collectives  95 us (9%)
  matrix products  34.2 us (3%)
  local copies, waits for them, and re-layouts  29.3 us (3%)
  between operations  15.1 us (1%)
  other arithmetic  13.8 us (1%)
    psum x5, waiting for transfers between devices, per_device(): lax.psum(jnp.dot(g_share, rows_half, preferred_element_type=jnp.float32)....  324 us
    psum x4, waiting for transfers between devices, per_device(): lax.psum(jnp.einsum('up,ur->pr', c_share, from_above, preferred_element_t...  252 us
    ppermute x45, waiting for transfers between devices, partner(): return lax.ppermute(block, axis, route)  128 us
    ppermute x45, starting transfers between devices, partner(): return lax.ppermute(block, axis, route)  96.3 us
    all_to_all x4, blocking collectives, per_device(): lax.all_to_all(outgoing, 'front', split_axis=0, concat_axis=0, tiled=True)  95 us
    all_gather x5, waiting for transfers between devices, per_device(): lax.all_gather(jnp.stack([carried, sibling]), 'front', axis=1, tiled=True)  89.7 us
  transfers between devices with their start and end apart: 60, of which 60 were waited for; matrix products, arithmetic and copies ran while one was open for 1% of the time, Pallas kernels for 0%

commit v1 on v0

--- a/solution.py
+++ b/solution.py
@@ -1,3 +1,4 @@
+import functools
 import jax
 import jax.numpy as jnp
 from jax import lax
@@ -6,6 +7,13 @@
 PIV = 4096
 UPD = 1024
 BLK = 128
+
+
+def replace_table_up(u_in, chip_axis):
+    return lax.all_gather(u_in, axis_name=chip_axis).sum(axis=0)
+
+
+paths_name = functools.partial(replace_table_up, chip_axis="front")
 
 
 def partner(block, axis, stride):
@@ -112,9 +120,8 @@
         own_rows = gather_own(upper_rhs[rhs_start : rhs_start + rhs_len], height, position)
         rows_half = (own_rows + assembled[:piv_dev]).astype(jnp.bfloat16)
         g_share = pivot_inverse[band_start : band_start + span_rows]
-        pivot_part = lax.psum(
-            jnp.dot(g_share, rows_half, preferred_element_type=jnp.float32).astype(jnp.bfloat16),
-            "front",
+        pivot_part = paths_name(
+            jnp.dot(g_share, rows_half, preferred_element_type=jnp.float32).astype(jnp.bfloat16)
         ).astype(jnp.float32)
         pivot_half = pivot_part.astype(jnp.bfloat16)
         saved_part.append(pivot_part)

time: 1100 us -> 996 us (0.905)
  waiting for transfers between devices: 799 us -> 625 us
  local copies, waits for them, and re-layouts: 29.3 us -> 73.7 us
  other arithmetic: 13.8 us -> 39.8 us
    psum x5 -> x0, waiting for transfers between devices: 324 us -> none  [per_device(): lax.psum(jnp.dot(g_share, rows_half, preferred_element_type=jnp.float32)....]
    all_gather x0 -> x4, waiting for transfers between devices: none -> 143 us  [replace_table_up(): return lax.all_gather(u_in, axis_name=chip_axis).sum(axis=0)]
    unnamed x22 -> x49, local copies, waits for them, and re-layouts: 2.15 us -> 31.1 us
    all_gather x0 -> x1, blocking collectives: none -> 18.3 us  [replace_table_up(): return lax.all_gather(u_in, axis_name=chip_axis).sum(axis=0)]
    reduce_sum x0 -> x5, other arithmetic: none -> 16.6 us  [replace_table_up(): return lax.all_gather(u_in, axis_name=chip_axis).sum(axis=0)]
    ppermute x45, waiting for transfers between devices: 128 us -> 144 us  [partner(): return lax.ppermute(block, axis, route)]
    all_to_all x4, blocking collectives: 95 us -> 79.5 us  [per_device(): lax.all_to_all(outgoing, 'front', split_axis=0, concat_axis=0, tiled=True)]
  transfers between devices with their start and end apart: 60 -> 59, of which waited for: 60 -> 57; matrix products, arithmetic and copies ran while one was open for 1% -> 2% of each run, Pallas kernels for 0% -> 0%
where the time goes in v1:
time: 996 us; the launch traced here: 992 us
  waiting for transfers between devices  625 us (63%)
  starting transfers between devices  104 us (10%)
  blocking collectives  97.8 us (10%)
  local copies, waits for them, and re-layouts  73.7 us (7%)
  other arithmetic  39.8 us (4%)
  matrix products  36 us (4%)
  between operations  15.1 us (2%)
    psum x4, waiting for transfers between devices, per_device(): lax.psum(jnp.einsum('up,ur->pr', c_share, from_above, preferred_element_t...  252 us
    ppermute x45, waiting for transfers between devices, partner(): return lax.ppermute(block, axis, route)  144 us
    all_gather x4, waiting for transfers between devices, replace_table_up(): return lax.all_gather(u_in, axis_name=chip_axis).sum(axis=0)  143 us
    ppermute x45, starting transfers between devices, partner(): return lax.ppermute(block, axis, route)  94 us
    all_gather x5, waiting for transfers between devices, per_device(): lax.all_gather(jnp.stack([carried, sibling]), 'front', axis=1, tiled=True)  81.7 us
    all_to_all x4, blocking collectives, per_device(): lax.all_to_all(outgoing, 'front', split_axis=0, concat_axis=0, tiled=True)  79.5 us
    unnamed x49, local copies, waits for them, and re-layouts  31.1 us
  transfers between devices with their start and end apart: 59, of which 57 were waited for; matrix products, arithmetic and copies ran while one was open for 2% of the time, Pallas kernels for 0%

profile of v1, /device:TPU:1, one launch (start us, length us, event | category | flops | bytes accessed | tf_op | source)
XLA Modules:
  0.0 991.6 jit_solution(3074532002690835983)
XLA Ops:
  18.2 25.2 %all-gather.15.cloned.1.call-done = bf16[2,1024,256]{2,1,0:T(8,128)(2,1)} async-done(((bf16[2,128,256]{2,1,0:T(8,128)(2,1)}), bf16[2,1024,256]{2,1,0:T(8,128)(2,1)}) %all-gather.15.cloned.1.call-update) | async-done | bytes 1048592 | tf_op jit(solution)/shard_map/all_gather | solution.py:108
  50.7 51.7 %all-gather.25.cloned.1.call-done = bf16[16384,256]{0,1:T(8,128)(2,1)} async-done(((bf16[2048,256]{0,1:T(8,128)(2,1)}), bf16[16384,256]{0,1:T(8,128)(2,1)}) %all-gather.25.cloned.1.call-update) | async-done | bytes 8388624 | tf_op jit(solution)/shard_map/all_gather | solution.py:13
  102.4 16.2 %copy.73 = bf16[32,8,8,2048]{3,2,1,0:T(8,128)(2,1)} copy(bf16[32,8,8,2048]{3,1,2,0:T(8,128)(2,1)} %bitcast.96) | data formatting | bytes 16777216
  118.6 10.4 %bitcast_reduce_fusion = bf16[2048,256]{0,1:T(8,128)(2,1)S(1)} fusion(bf16[32,8,8,2048]{3,2,1,0:T(8,128)(2,1)} %copy.73), kind=kLoop, calls=%fused_computation.5 | loop fusion | flops 3670016 | bytes 9437184 | tf_op jit(solution)/shard_map/reduce_sum | solution.py:13
  148.0 18.6 %all-gather.17.cloned.1.call-done = bf16[2,1024,256]{1,2,0:T(8,128)(2,1)} async-done(((bf16[2,128,256]{1,2,0:T(8,128)(2,1)}), bf16[2,1024,256]{1,2,0:T(8,128)(2,1)}) %all-gather.17.cloned.1.call-update) | async-done | bytes 1048592 | tf_op jit(solution)/shard_map/all_gather | solution.py:108
  175.4 35.5 %all-gather.27.cloned.1.call-done = bf16[8192,256]{0,1:T(8,128)(2,1)} async-done(((bf16[1024,256]{0,1:T(8,128)(2,1)}), bf16[8192,256]{0,1:T(8,128)(2,1)}) %all-gather.27.cloned.1.call-update) | async-done | bytes 4194320 | tf_op jit(solution)/shard_map/all_gather | solution.py:13
  210.8 6.5 copy.74
  248.7 16.5 %all-gather.19.cloned.1.call-done = bf16[2,1024,256]{1,2,0:T(8,128)(2,1)} async-done(((bf16[2,128,256]{1,2,0:T(8,128)(2,1)}), bf16[2,1024,256]{1,2,0:T(8,128)(2,1)}) %all-gather.19.cloned.1.call-update) | async-done | bytes 1048592 | tf_op jit(solution)/shard_map/all_gather | solution.py:108
  273.3 28.9 %all-gather.29.cloned.1.call-done = bf16[4096,256]{0,1:T(8,128)(2,1)} async-done(((bf16[512,256]{0,1:T(8,128)(2,1)}), bf16[4096,256]{0,1:T(8,128)(2,1)}) %all-gather.29.cloned.1.call-update) | async-done | bytes 2097168 | tf_op jit(solution)/shard_map/all_gather | solution.py:13
  343.8 13.7 %all-gather.21.cloned.1.call-done = bf16[2,1024,256]{1,2,0:T(8,128)(2,1)} async-done(((bf16[2,128,256]{1,2,0:T(8,128)(2,1)}), bf16[2,1024,256]{1,2,0:T(8,128)(2,1)}) %all-gather.21.cloned.1.call-update) | async-done | bytes 1048592 | tf_op jit(solution)/shard_map/all_gather | solution.py:108
  365.6 26.7 %all-gather.31.cloned.1.call-done = bf16[2048,256]{0,1:T(8,128)(2,1)} async-done(((bf16[256,256]{0,1:T(8,128)(2,1)}), bf16[2048,256]{0,1:T(8,128)(2,1)}) %all-gather.31.cloned.1.call-update) | async-done | bytes 1048592 | tf_op jit(solution)/shard_map/all_gather | solution.py:13
  413.4 6.2 collective-permute-start.29
  437.7 5.3 collective-permute-start.24
  447.1 7.8 all-gather.23.cloned.1.call-done
  460.9 18.3 %all-gather.4 = bf16[1024,256]{0,1:T(8,128)(2,1)S(1)} all-gather(bf16[128,256]{0,1:T(8,128)(2,1)S(1)} %fusion.14), channel_id=6, replica_groups=mesh['leaf'=32,'front'=8] {'front'}, dimensions={0}, use_global_device_ids=true | all-gather | bytes 589824 | tf_op jit(solution)/shard_map/all_gather | solution.py:13
  482.0 6.7 collective-permute-done.30
  491.4 5.8 collective-permute-done.31
  497.4 6.0 collective-permute-done.32
  504.8 13.7 %collective-permute-done.33 = bf16[512,256]{0,1:T(8,128)(2,1)S(1)} collective-permute-done((bf16[512,256]{0,1:T(8,128)(2,1)S(1)}, bf16[512,256]{0,1:T(8,128)(2,1)S(1)}, u32[]{:S(2)}, u32[]{:S(2)}) %collective-permute-start.33) | collective-permute-done | bytes 262176 | tf_op jit(solution)/shard_map/ppermute | solution.py:26
  523.2 12.4 %collective-permute-done.34 = bf16[512,256]{0,1:T(8,128)(2,1)S(1)} collective-permute-done((bf16[512,256]{0,1:T(8,128)(2,1)S(1)}, bf16[512,256]{0,1:T(8,128)(2,1)S(1)}, u32[]{:S(2)}, u32[]{:S(2)}) %collective-permute-start.34) | collective-permute-done | bytes 262176 | tf_op jit(solution)/shard_map/ppermute | solution.py:26
  539.3 13.7 %all_to_all.25 = bf16[8,128,256]{2,1,0:T(8,128)(2,1)S(1)} all-to-all(bf16[8,128,256]{2,1,0:T(8,128)(2,1)S(1)} %copy.50), channel_id=1, replica_groups=mesh['leaf'=32,'front'=8] {'front'}, dimensions={0} | all-to-all | bytes 1048576 | tf_op jit(solution)/shard_map/all_to_all | solution.py:174
  554.0 59.7 %all-reduce.6.cloned.1.call-done = bf16[256,256]{0,1:T(8,128)(2,1)} async-done(((bf16[256,256]{0,1:T(8,128)(2,1)}), bf16[256,256]{0,1:T(8,128)(2,1)}) %all-reduce.6.cloned.1.call-update) | async-done | bytes 131088 | tf_op jit(solution)/shard_map/psum | solution.py:144
  623.1 5.4 collective-permute-done.36
  637.2 6.9 collective-permute-done.38
  648.9 24.9 %all_to_all.26 = bf16[8,128,256]{2,1,0:T(8,128)(2,1)S(1)} all-to-all(bf16[8,128,256]{2,1,0:T(8,128)(2,1)S(1)} %copy.54), channel_id=1, replica_groups=mesh['leaf'=32,'front'=8] {'front'}, dimensions={0} | all-to-all | bytes 1048576 | tf_op jit(solution)/shard_map/all_to_all | solution.py:174
  674.9 62.8 %all-reduce.8.cloned.1.call-done = bf16[512,256]{0,1:T(8,128)(2,1)} async-done(((bf16[512,256]{0,1:T(8,128)(2,1)}), bf16[512,256]{0,1:T(8,128)(2,1)}) %all-reduce.8.cloned.1.call-update) | async-done | bytes 262160 | tf_op jit(solution)/shard_map/psum | solution.py:144
  747.2 5.4 collective-permute-done.40
  764.4 20.9 %all_to_all.27 = bf16[8,128,256]{2,1,0:T(8,128)(2,1)S(1)} all-to-all(bf16[8,128,256]{2,1,0:T(8,128)(2,1)S(1)} %copy.58), channel_id=1, replica_groups=mesh['leaf'=32,'front'=8] {'front'}, dimensions={0} | all-to-all | bytes 1048576 | tf_op jit(solution)/shard_map/all_to_all | solution.py:174
  786.5 63.8 %all-reduce.10.cloned.1.call-done = bf16[1024,256]{0,1:T(8,128)(2,1)} async-done(((bf16[1024,256]{0,1:T(8,128)(2,1)}), bf16[1024,256]{0,1:T(8,128)(2,1)}) %all-reduce.10.cloned.1.call-update) | async-done | bytes 524304 | tf_op jit(solution)/shard_map/psum | solution.py:144
  869.4 20.0 %all_to_all.28 = bf16[8,128,256]{2,1,0:T(8,128)(2,1)S(1)} all-to-all(bf16[8,128,256]{2,1,0:T(8,128)(2,1)S(1)} %copy.62), channel_id=1, replica_groups=mesh['leaf'=32,'front'=8] {'front'}, dimensions={0} | all-to-all | bytes 1048576 | tf_op jit(solution)/shard_map/all_to_all | solution.py:174
  890.9 65.6 %all-reduce.12.cloned.1.call-done = bf16[2048,256]{0,1:T(8,128)(2,1)} async-done(((bf16[2048,256]{0,1:T(8,128)(2,1)}), bf16[2048,256]{0,1:T(8,128)(2,1)}) %all-reduce.12.cloned.1.call-update) | async-done | bytes 1048592 | tf_op jit(solution)/shard_map/psum | solution.py:144
  966.5 8.3 all-to-all-start.4
  (337 shorter events, 287.2 us)
Async XLA Ops:
  7.2 36.2 %all-gather.15.cloned.1.call-start = ((), (), s32[]{:S(2)}) async-start(), calls=%async_computation.5 | async-start | bytes 1179648 | tf_op jit(solution)/shard_map/all_gather | solution.py:108
  12.8 89.6 %all-gather.25.cloned.1.call-start = ((), (), s32[]{:S(2)}) async-start(), calls=%async_computation.14 | async-start | bytes 9437184 | tf_op jit(solution)/shard_map/all_gather | solution.py:13
  50.2 116.4 %all-gather.17.cloned.1.call-start = ((), (), s32[]{:S(2)}) async-start(), calls=%async_computation.6 | async-start | bytes 1179648 | tf_op jit(solution)/shard_map/all_gather | solution.py:108
  138.1 72.7 %all-gather.27.cloned.1.call-start = ((), (), s32[]{:S(2)}) async-start(), calls=%async_computation.15 | async-start | bytes 4718592 | tf_op jit(solution)/shard_map/all_gather | solution.py:13
  142.1 5.8 collective-permute-start.3
  175.1 90.0 %all-gather.19.cloned.1.call-start = ((), (), s32[]{:S(2)}) async-start(), calls=%async_computation.7 | async-start | bytes 1179648 | tf_op jit(solution)/shard_map/all_gather | solution.py:108
  235.7 66.5 %all-gather.29.cloned.1.call-start = ((), (), s32[]{:S(2)}) async-start(), calls=%async_computation.16 | async-start | bytes 2359296 | tf_op jit(solution)/shard_map/all_gather | solution.py:13
  273.2 84.3 %all-gather.21.cloned.1.call-start = ((), (), s32[]{:S(2)}) async-start(), calls=%async_computation.8 | async-start | bytes 1179648 | tf_op jit(solution)/shard_map/all_gather | solution.py:108
  325.8 66.5 %all-gather.31.cloned.1.call-start = ((), (), s32[]{:S(2)}) async-start(), calls=%async_computation.17 | async-start | bytes 1179648 | tf_op jit(solution)/shard_map/all_gather | solution.py:13
  337.1 6.7 collective-permute-start.15
  365.4 89.5 %all-gather.23.cloned.1.call-start = ((), (), s32[]{:S(2)}) async-start(), calls=%async_computation.9 | async-start | bytes 1179648 | tf_op jit(solution)/shard_map/all_gather | solution.py:108
  413.4 8.0 collective-permute-start.29
  422.1 191.7 %all-reduce.6.cloned.1.call-start = ((), (), s32[]{:S(2)}) async-start(), calls=%async_computation.10 | async-start | bytes 262144 | tf_op jit(solution)/shard_map/psum | solution.py:144
  437.7 8.7 collective-permute-start.24
  480.9 7.8 collective-permute-start.30
  488.8 8.4 collective-permute-start.31
  497.3 6.1 collective-permute-start.32
  503.5 15.0 %collective-permute-start.33 = (bf16[512,256]{0,1:T(8,128)(2,1)S(1)}, bf16[512,256]{0,1:T(8,128)(2,1)S(1)}, u32[]{:S(2)}, u32[]{:S(2)}) collective-permute-start(bf16[512,256]{0,1:T(8,128)(2,1)S(1)} %fusion.32), channel_id=1, source_target_pairs={{0,64},{64,0},{8,72},{72,8},{16,80},{80,16},{24,88},{88,24},{32,96... | collective-permute-start | bytes 786440 | tf_op jit(solution)/shard_map/ppermute | solution.py:26
  518.6 17.0 %collective-permute-start.34 = (bf16[512,256]{0,1:T(8,128)(2,1)S(1)}, bf16[512,256]{0,1:T(8,128)(2,1)S(1)}, u32[]{:S(2)}, u32[]{:S(2)}) collective-permute-start(bf16[512,256]{0,1:T(8,128)(2,1)S(1)} %fusion.51), channel_id=1, source_target_pairs={{0,128},{128,0},{8,136},{136,8},{16,144},{144,16},{24,152},{152,24... | collective-permute-start | bytes 786440 | tf_op jit(solution)/shard_map/ppermute | solution.py:26
  554.0 183.7 %all-reduce.8.cloned.1.call-start = ((), (), s32[]{:S(2)}) async-start(), calls=%async_computation.11 | async-start | bytes 524288 | tf_op jit(solution)/shard_map/psum | solution.py:144
  615.0 5.3 collective-permute-start.35
  620.4 8.2 collective-permute-start.36
  628.6 5.3 collective-permute-start.37
  634.8 9.2 collective-permute-start.38
  674.8 175.5 %all-reduce.10.cloned.1.call-start = ((), (), s32[]{:S(2)}) async-start(), calls=%async_computation.12 | async-start | bytes 1048576 | tf_op jit(solution)/shard_map/psum | solution.py:144
  744.5 8.2 collective-permute-start.40
  754.1 5.5 collective-permute-start.41
  786.5 170.1 %all-reduce.12.cloned.1.call-start = ((), (), s32[]{:S(2)}) async-start(), calls=%async_computation.13 | async-start | bytes 2097152 | tf_op jit(solution)/shard_map/psum | solution.py:144
  852.2 5.3 collective-permute-start.42
  858.3 7.5 collective-permute-start.43
  959.2 5.3 collective-permute-start.44
  966.5 17.6 %all-to-all-start.4 = ((bf16[8,128,256]{2,1,0:T(8,128)(2,1)}), bf16[8,128,256]{2,1,0:T(8,128)(2,1)S(1)}, u32[]{:S(2)}, u32[]{:S(2)}) async-start(bf16[8,128,256]{2,1,0:T(8,128)(2,1)} %copy.66), calls=%async_computation.4 | async-start | bytes 1048576 | tf_op jit(solution)/shard_map/all_to_all | solution.py:174
  (53 other events, 934.0 us)
Sparse Core Ops, SparseCore 0:
  12.9 30.4 all-gather.14
  50.3 52.0 all-gather.24
  138.2 28.2 all-gather.16
  175.2 35.5 all-gather.26
  235.8 29.2 all-gather.18
  273.3 28.7 all-gather.28
  326.0 31.4 all-gather.20
  365.5 26.7 all-gather.30
  422.2 32.6 all-gather.22
  554.1 59.6 all-reduce.5
  674.9 62.6 all-reduce.7
  786.6 63.7 all-reduce.9
  891.1 65.4 all-reduce.11
